TPU v7x, 512 devices: a whole 4x8x8 slice. The times are simulated.
512 devices in a mesh: mod: 512 (over y, z, x, core).
Axes of the slice: x: 4, y: 8, z: 8, core: 2. Of those that a mesh axis runs over, the one named last changes fastest.
Arguments:
- loads: bfloat16 [32, 524288], P(None, 'mod')
- modes: float32 [6, 524288], P(None, 'mod'), may hold values from -0.6 to 0.6
- pinv: bfloat16 [524288, 1024], P('mod')
- schur: bfloat16 [524288, 1024], P('mod')
- coarse_inverse: float32 [3072, 3072], P('mod')
- connectors: int32 [512, 3, 8], P('mod'), may hold values from -1 to 4, as said below
Outputs:
- multipliers: float32 [32, 524288], P(None, 'mod')
Inputs may be any that keep to these rules, and one draw needn't show every extreme that they name: connectors[s, 0, b] is 0 for an unused block, or 1, 2, 3, 4 when the block is tied to module s + 1, s - 1, s + 8, s - 8; its partner is the block of that module with the opposite direction (1 with 2, 3 with 4) and the same slot connectors[s, 1, b], which is below 2 (0 on unused blocks). connectors[s, 2, b] is +1 or -1 on used blocks, opposite at the two ends of a connector, and 0 on unused ones. Partners stay within rows of 8 modules along the first kind of direction and within the modules along the second. A module uses at most 2 blocks towards one neighbour, and some module uses 2.
All inputs are finite; a program needn't handle non-finite values.
Results may differ from a plain program's by a relative error of at most 0.0015.
Values sent between devices are 32-bit elements; how exact they have to be, the bound alone decides.
A program may use at most 64 MiB of HBM per device.

v0:
```python
import jax
import jax.numpy as jnp
from jax import lax
from jax.sharding import PartitionSpec as P

MODES = 6
MAXC = 2
ACROSS = 8
highest = lax.Precision.HIGHEST


def shifted(block, axis, distance):
    devices = range(lax.axis_size(axis))
    route = [(i - distance, i) for i in devices if i - distance in devices]
    return lax.ppermute(block, axis, route)


def on_device(loads, modes, pinv, schur, coarse_inverse, connectors):
    case_count, dof_count = loads.shape
    block_count = connectors.shape[2]
    block_size = dof_count // block_count
    orient = connectors[0, 2].astype(jnp.float32)
    orient_flat = jnp.repeat(orient, block_size)[None, :]
    headings = connectors[0, 0]
    slot_ids = connectors[0, 1]
    heading_ids = jnp.arange(4, dtype=jnp.int32)[:, None, None] + 1
    slot_range = jnp.arange(MAXC, dtype=jnp.int32)[None, :, None]
    selector = (
        (headings[None, None] == heading_ids) & (slot_ids[None, None] == slot_range)
    ).astype(jnp.float32)
    offsets = [1, -1, ACROSS, -ACROSS]
    module_count = coarse_inverse.shape[1] // MODES
    inverse_view = coarse_inverse.reshape(MODES, module_count, MODES)

    def jump_with(values_in, mover):
        signed = values_in.reshape(case_count, block_count, block_size) * orient[None, :, None]
        summed = signed
        for heading in range(4):
            packed = jnp.einsum("kb,cbe->kce", selector[heading ^ 1], signed, precision=highest)
            received = mover(packed, heading)
            summed = summed + jnp.einsum(
                "kb,kce->cbe", selector[heading], received, precision=highest
            )
        return summed.reshape(case_count, dof_count)

    def move_values(packed, heading):
        return shifted(packed, "mod", -offsets[heading])

    def move_lifted(packed, heading):
        return shifted(packed, "mod", -offsets[heading])

    def apply_jump(values_in):
        return jump_with(values_in, move_values)

    def coarse_rhs(values_in):
        return lax.dot_general(modes, values_in, (((1,), (1,)), ((), ())), precision=highest)

    def lift(amplitude):
        return lax.dot_general(amplitude, modes, (((0,), (0,)), ((), ())), precision=highest)

    def jump_lift(amplitude):
        return jump_with(lift(amplitude), move_lifted)

    def absorb(piece):
        amplitude = jnp.einsum("imj,mjc->ic", inverse_view, piece, precision=highest)
        return (amplitude, jnp.sum(piece[:, MODES:], axis=(0, 1)))

    def coarse_solve(right_side, partial_value):
        amplitude, unused = absorb(lax.all_gather(right_side[None], "mod", axis=0, tiled=True))
        total_rho = None if partial_value is None else lax.psum(partial_value, "mod")
        return (amplitude, total_rho)

    def project(values_in, partial_value):
        amplitude, total_rho = coarse_solve(coarse_rhs(orient_flat * values_in), partial_value)
        return (values_in - jump_lift(amplitude), total_rho)

    load_values = loads.astype(jnp.float32)
    first_amplitude, unused_rho = coarse_solve(coarse_rhs(load_values), None)
    multipliers = jump_lift(first_amplitude)
    start = (load_values - orient_flat * multipliers).astype(jnp.bfloat16)
    residual = apply_jump(jnp.dot(start, pinv, preferred_element_type=jnp.float32))
    projected, unused_total = project(residual, None)
    scaled = (orient_flat * projected).astype(jnp.bfloat16)
    smoothed = jnp.dot(scaled, schur, preferred_element_type=jnp.float32)
    partial_value = jnp.sum(scaled.astype(jnp.float32) * smoothed, axis=1)
    corrected, rho = project(apply_jump(smoothed), partial_value)
    lifted = (orient_flat * corrected).astype(jnp.bfloat16)
    response = jnp.dot(lifted, pinv, preferred_element_type=jnp.float32)
    kappa = lax.psum(jnp.sum(lifted.astype(jnp.float32) * response, axis=1), "mod")
    stride = rho / kappa
    multipliers = multipliers + stride[:, None] * corrected
    return multipliers


def solution(mesh):
    in_specs = (
        P(None, "mod"),
        P(None, "mod"),
        P("mod", None),
        P("mod", None),
        P("mod", None),
        P("mod", None, None),
    )
    out_specs = P(None, "mod")
    return jax.shard_map(
        on_device, mesh=mesh, in_specs=in_specs, out_specs=out_specs, check_vma=False
    )
```

profile of v0, /device:TPU:1, one launch (start us, length us, event | category | flops | bytes accessed | tf_op | source)
XLA Modules:
  0.0 439.6 jit_solution(2911055395956350459)
XLA Ops:
  0.9 3.7 reshape.144
  4.6 2.0 copy.8
  6.8 79.2 %all-gather.3 = f32[512,6,32]{2,1,0:T(8,128)S(1)} all-gather(f32[1,6,32]{2,1,0:T(8,128)S(1)} %convolution_bitcast_fusion.22), channel_id=2, replica_groups=mesh['mod'=512] {'mod'}, dimensions={0}, use_global_device_ids=true | all-gather | bytes 393984 | tf_op jit(solution)/shard_map/all_gather | solution.py:69
  87.8 2.1 collective-permute-start
  90.0 3.5 collective-permute-start.1
  95.2 4.0 collective-permute-start.3
  102.6 3.6 collective-permute-start.7
  106.4 3.3 collective-permute-start.4
  109.8 2.2 collective-permute-start.5
  112.0 1.3 collective-permute-start.6
  113.6 3.1 collective-permute-done.6
  117.6 86.2 %all-gather.4 = f32[512,6,32]{2,1,0:T(8,128)S(1)} all-gather(f32[1,6,32]{2,1,0:T(8,128)S(1)} %convolution_bitcast_fusion.21), channel_id=3, replica_groups=mesh['mod'=512] {'mod'}, dimensions={0}, use_global_device_ids=true | all-gather | bytes 393984 | tf_op jit(solution)/shard_map/all_gather | solution.py:69
  207.5 2.1 collective-permute-start.8
  209.6 3.5 collective-permute-start.9
  213.1 1.3 collective-permute-start.10
  214.7 3.1 collective-permute-done.10
  220.1 2.0 collective-permute-start.12
  222.0 3.6 collective-permute-start.13
  226.9 4.0 collective-permute-start.15
  233.2 86.6 %all-gather.5 = f32[512,6,32]{2,1,0:T(8,128)S(1)} all-gather(f32[1,6,32]{2,1,0:T(8,128)S(1)} %convolution_bitcast_fusion.20), channel_id=4, replica_groups=mesh['mod'=512] {'mod'}, dimensions={0}, use_global_device_ids=true | all-gather | bytes 393984 | tf_op jit(solution)/shard_map/all_gather | solution.py:69
  323.5 2.1 collective-permute-start.16
  325.6 3.5 collective-permute-start.17
  330.7 3.1 collective-permute-done.18
  335.1 103.7 %all-reduce = (f32[32]{0:T(128)S(1)}, f32[32]{0:T(128)S(1)}) all-reduce(f32[32]{0:T(128)S(1)} %get-tuple-element.8, f32[32]{0:T(128)S(1)} %fusion.26), channel_id=1, replica_groups=mesh['mod'=512] {'mod'}, use_global_device_ids=true, to_apply=%region_1.0 | all-reduce | flops 64 | bytes 512 | tf_op jit(solution)/shard_map/psum | solution.py:70
  (111 shorter events, 26.0 us)
Async XLA Ops:
  0.0 101.3 %copy-start = (bf16[1024,1024]{1,0:T(8,128)(2,1)S(1)}, bf16[1024,1024]{1,0:T(8,128)(2,1)}, u32[]{:S(2)}) copy-start(bf16[1024,1024]{1,0:T(8,128)(2,1)} %param.8) | copy-start | bytes 6291460
  0.0 6.6 %copy-start.2 = (f32[6,1024]{1,0:T(8,128)S(1)}, f32[6,1024]{1,0:T(8,128)}, u32[]{:S(2)}) copy-start(f32[6,1024]{1,0:T(8,128)} %param.7) | copy-start | bytes 73732
  0.0 6.7 %copy-start.3 = (bf16[32,1024]{1,0:T(8,128)(2,1)S(1)}, bf16[32,1024]{1,0:T(8,128)(2,1)}, u32[]{:S(2)}) copy-start(bf16[32,1024]{1,0:T(8,128)(2,1)} %param.6) | copy-start | bytes 196612
  87.8 13.3 %collective-permute-start = (f32[2,32,128]{2,0,1:T(2,128)S(1)}, f32[2,32,128]{2,0,1:T(2,128)S(1)}, u32[]{:S(2)}, u32[]{:S(2)}) collective-permute-start(f32[2,32,128]{2,0,1:T(2,128)S(1)} %fusion.52), channel_id=1, source_target_pairs={{1,0},{2,1},{3,2},{4,3},{5,4},{6,5},{7,6},{8,7},{9,8},{10,9},{11,1... | collective-permute-start | bytes 98312 | tf_op jit(solution)/shard_map/ppermute | solution.py:15
  90.0 10.7 %collective-permute-start.1 = (f32[2,32,128]{2,0,1:T(2,128)S(1)}, f32[2,32,128]{2,0,1:T(2,128)S(1)}, u32[]{:S(2)}, u32[]{:S(2)}) collective-permute-start(f32[2,32,128]{2,0,1:T(2,128)S(1)} %fusion.57), channel_id=1, source_target_pairs={{0,1},{1,2},{2,3},{3,4},{4,5},{5,6},{6,7},{7,8},{8,9},{9,10},{10,1... | collective-permute-start | bytes 98312 | tf_op jit(solution)/shard_map/ppermute | solution.py:15
  93.7 6.8 %collective-permute-start.2 = (f32[2,32,128]{2,0,1:T(2,128)S(1)}, f32[2,32,128]{2,0,1:T(2,128)S(1)}, u32[]{:S(2)}, u32[]{:S(2)}) collective-permute-start(f32[2,32,128]{2,0,1:T(2,128)S(1)} %fusion.62), channel_id=1, source_target_pairs={{8,0},{9,1},{10,2},{11,3},{12,4},{13,5},{14,6},{15,7},{16,8},{17,9... | collective-permute-start | bytes 98312 | tf_op jit(solution)/shard_map/ppermute | solution.py:15
  95.2 5.0 %collective-permute-start.3 = (f32[2,32,128]{2,0,1:T(2,128)S(1)}, f32[2,32,128]{2,0,1:T(2,128)S(1)}, u32[]{:S(2)}, u32[]{:S(2)}) collective-permute-start(f32[2,32,128]{2,0,1:T(2,128)S(1)} %fusion.67), channel_id=1, source_target_pairs={{0,8},{1,9},{2,10},{3,11},{4,12},{5,13},{6,14},{7,15},{8,16},{9,17... | collective-permute-start | bytes 98312 | tf_op jit(solution)/shard_map/ppermute | solution.py:15
  102.6 10.7 %collective-permute-start.7 = (f32[2,32,128]{2,0,1:T(2,128)S(1)}, f32[2,32,128]{2,0,1:T(2,128)S(1)}, u32[]{:S(2)}, u32[]{:S(2)}) collective-permute-start(f32[2,32,128]{2,0,1:T(2,128)S(1)} %fusion.66), channel_id=1, source_target_pairs={{0,8},{1,9},{2,10},{3,11},{4,12},{5,13},{6,14},{7,15},{8,16},{9,17... | collective-permute-start | bytes 98312 | tf_op jit(solution)/shard_map/ppermute | solution.py:15
  106.4 10.8 %collective-permute-start.4 = (f32[2,32,128]{2,0,1:T(2,128)S(1)}, f32[2,32,128]{2,0,1:T(2,128)S(1)}, u32[]{:S(2)}, u32[]{:S(2)}) collective-permute-start(f32[2,32,128]{2,0,1:T(2,128)S(1)} %fusion.51), channel_id=1, source_target_pairs={{1,0},{2,1},{3,2},{4,3},{5,4},{6,5},{7,6},{8,7},{9,8},{10,9},{11,1... | collective-permute-start | bytes 98312 | tf_op jit(solution)/shard_map/ppermute | solution.py:15
  109.8 7.2 %collective-permute-start.5 = (f32[2,32,128]{2,0,1:T(2,128)S(1)}, f32[2,32,128]{2,0,1:T(2,128)S(1)}, u32[]{:S(2)}, u32[]{:S(2)}) collective-permute-start(f32[2,32,128]{2,0,1:T(2,128)S(1)} %fusion.56), channel_id=1, source_target_pairs={{0,1},{1,2},{2,3},{3,4},{4,5},{5,6},{6,7},{7,8},{8,9},{9,10},{10,1... | collective-permute-start | bytes 98312 | tf_op jit(solution)/shard_map/ppermute | solution.py:15
  112.0 4.7 %collective-permute-start.6 = (f32[2,32,128]{2,0,1:T(2,128)S(1)}, f32[2,32,128]{2,0,1:T(2,128)S(1)}, u32[]{:S(2)}, u32[]{:S(2)}) collective-permute-start(f32[2,32,128]{2,0,1:T(2,128)S(1)} %fusion.61), channel_id=1, source_target_pairs={{8,0},{9,1},{10,2},{11,3},{12,4},{13,5},{14,6},{15,7},{16,8},{17,9... | collective-permute-start | bytes 98312 | tf_op jit(solution)/shard_map/ppermute | solution.py:15
  204.9 13.7 %copy-start.1 = (bf16[1024,1024]{1,0:T(8,128)(2,1)S(1)}, bf16[1024,1024]{1,0:T(8,128)(2,1)}, u32[]{:S(2)}) copy-start(bf16[1024,1024]{1,0:T(8,128)(2,1)} %param.9) | copy-start | bytes 6291460
  206.0 8.4 %collective-permute-start.11 = (f32[2,32,128]{2,0,1:T(2,128)S(1)}, f32[2,32,128]{2,0,1:T(2,128)S(1)}, u32[]{:S(2)}, u32[]{:S(2)}) collective-permute-start(f32[2,32,128]{2,0,1:T(2,128)S(1)} %fusion.65), channel_id=1, source_target_pairs={{0,8},{1,9},{2,10},{3,11},{4,12},{5,13},{6,14},{7,15},{8,16},{9,17... | collective-permute-start | bytes 98312 | tf_op jit(solution)/shard_map/ppermute | solution.py:15
  207.5 10.8 %collective-permute-start.8 = (f32[2,32,128]{2,0,1:T(2,128)S(1)}, f32[2,32,128]{2,0,1:T(2,128)S(1)}, u32[]{:S(2)}, u32[]{:S(2)}) collective-permute-start(f32[2,32,128]{2,0,1:T(2,128)S(1)} %fusion.50), channel_id=1, source_target_pairs={{1,0},{2,1},{3,2},{4,3},{5,4},{6,5},{7,6},{8,7},{9,8},{10,9},{11,1... | collective-permute-start | bytes 98312 | tf_op jit(solution)/shard_map/ppermute | solution.py:15
  209.6 8.4 %collective-permute-start.9 = (f32[2,32,128]{2,0,1:T(2,128)S(1)}, f32[2,32,128]{2,0,1:T(2,128)S(1)}, u32[]{:S(2)}, u32[]{:S(2)}) collective-permute-start(f32[2,32,128]{2,0,1:T(2,128)S(1)} %fusion.55), channel_id=1, source_target_pairs={{0,1},{1,2},{2,3},{3,4},{4,5},{5,6},{6,7},{7,8},{8,9},{9,10},{10,1... | collective-permute-start | bytes 98312 | tf_op jit(solution)/shard_map/ppermute | solution.py:15
  213.1 4.7 %collective-permute-start.10 = (f32[2,32,128]{2,0,1:T(2,128)S(1)}, f32[2,32,128]{2,0,1:T(2,128)S(1)}, u32[]{:S(2)}, u32[]{:S(2)}) collective-permute-start(f32[2,32,128]{2,0,1:T(2,128)S(1)} %fusion.60), channel_id=1, source_target_pairs={{8,0},{9,1},{10,2},{11,3},{12,4},{13,5},{14,6},{15,7},{16,8},{17,9... | collective-permute-start | bytes 98312 | tf_op jit(solution)/shard_map/ppermute | solution.py:15
  220.1 12.7 %collective-permute-start.12 = (f32[2,32,128]{2,0,1:T(2,128)S(1)}, f32[2,32,128]{2,0,1:T(2,128)S(1)}, u32[]{:S(2)}, u32[]{:S(2)}) collective-permute-start(f32[2,32,128]{2,0,1:T(2,128)S(1)} %fusion.49), channel_id=1, source_target_pairs={{1,0},{2,1},{3,2},{4,3},{5,4},{6,5},{7,6},{8,7},{9,8},{10,9},{11,1... | collective-permute-start | bytes 98312 | tf_op jit(solution)/shard_map/ppermute | solution.py:15
  222.0 10.4 %collective-permute-start.13 = (f32[2,32,128]{2,0,1:T(2,128)S(1)}, f32[2,32,128]{2,0,1:T(2,128)S(1)}, u32[]{:S(2)}, u32[]{:S(2)}) collective-permute-start(f32[2,32,128]{2,0,1:T(2,128)S(1)} %fusion.54), channel_id=1, source_target_pairs={{0,1},{1,2},{2,3},{3,4},{4,5},{5,6},{6,7},{7,8},{8,9},{9,10},{10,1... | collective-permute-start | bytes 98312 | tf_op jit(solution)/shard_map/ppermute | solution.py:15
  225.6 6.6 %collective-permute-start.14 = (f32[2,32,128]{2,0,1:T(2,128)S(1)}, f32[2,32,128]{2,0,1:T(2,128)S(1)}, u32[]{:S(2)}, u32[]{:S(2)}) collective-permute-start(f32[2,32,128]{2,0,1:T(2,128)S(1)} %fusion.59), channel_id=1, source_target_pairs={{8,0},{9,1},{10,2},{11,3},{12,4},{13,5},{14,6},{15,7},{16,8},{17,9... | collective-permute-start | bytes 98312 | tf_op jit(solution)/shard_map/ppermute | solution.py:15
  226.9 5.0 %collective-permute-start.15 = (f32[2,32,128]{2,0,1:T(2,128)S(1)}, f32[2,32,128]{2,0,1:T(2,128)S(1)}, u32[]{:S(2)}, u32[]{:S(2)}) collective-permute-start(f32[2,32,128]{2,0,1:T(2,128)S(1)} %fusion.64), channel_id=1, source_target_pairs={{0,8},{1,9},{2,10},{3,11},{4,12},{5,13},{6,14},{7,15},{8,16},{9,17... | collective-permute-start | bytes 98312 | tf_op jit(solution)/shard_map/ppermute | solution.py:15
  322.0 8.4 %collective-permute-start.19 = (f32[2,32,128]{2,0,1:T(2,128)S(1)}, f32[2,32,128]{2,0,1:T(2,128)S(1)}, u32[]{:S(2)}, u32[]{:S(2)}) collective-permute-start(f32[2,32,128]{2,0,1:T(2,128)S(1)} %fusion.63), channel_id=1, source_target_pairs={{0,8},{1,9},{2,10},{3,11},{4,12},{5,13},{6,14},{7,15},{8,16},{9,17... | collective-permute-start | bytes 98312 | tf_op jit(solution)/shard_map/ppermute | solution.py:15
  323.5 10.8 %collective-permute-start.16 = (f32[2,32,128]{2,0,1:T(2,128)S(1)}, f32[2,32,128]{2,0,1:T(2,128)S(1)}, u32[]{:S(2)}, u32[]{:S(2)}) collective-permute-start(f32[2,32,128]{2,0,1:T(2,128)S(1)} %fusion.48), channel_id=1, source_target_pairs={{1,0},{2,1},{3,2},{4,3},{5,4},{6,5},{7,6},{8,7},{9,8},{10,9},{11,1... | collective-permute-start | bytes 98312 | tf_op jit(solution)/shard_map/ppermute | solution.py:15
  325.6 8.4 %collective-permute-start.17 = (f32[2,32,128]{2,0,1:T(2,128)S(1)}, f32[2,32,128]{2,0,1:T(2,128)S(1)}, u32[]{:S(2)}, u32[]{:S(2)}) collective-permute-start(f32[2,32,128]{2,0,1:T(2,128)S(1)} %fusion.53), channel_id=1, source_target_pairs={{0,1},{1,2},{2,3},{3,4},{4,5},{5,6},{6,7},{7,8},{8,9},{9,10},{10,1... | collective-permute-start | bytes 98312 | tf_op jit(solution)/shard_map/ppermute | solution.py:15
  329.1 4.7 %collective-permute-start.18 = (f32[2,32,128]{2,0,1:T(2,128)S(1)}, f32[2,32,128]{2,0,1:T(2,128)S(1)}, u32[]{:S(2)}, u32[]{:S(2)}) collective-permute-start(f32[2,32,128]{2,0,1:T(2,128)S(1)} %fusion.58), channel_id=1, source_target_pairs={{8,0},{9,1},{10,2},{11,3},{12,4},{13,5},{14,6},{15,7},{16,8},{17,9... | collective-permute-start | bytes 98312 | tf_op jit(solution)/shard_map/ppermute | solution.py:15
where the time goes:
time: 440 us
  blocking collectives  356 us (81%)
  starting transfers between devices  48.5 us (11%)
  matrix products  15.1 us (3%)
  waiting for transfers between devices  11.1 us (3%)
  local copies, waits for them, and re-layouts  6.04 us (1%)
    all_gather x3, blocking collectives, coarse_solve(): lax.all_gather(right_side[None], 'mod', axis=0, tiled=True)  252 us
    psum x1, blocking collectives, coarse_solve(): lax.psum(partial_value, 'mod')  104 us
    ppermute x20, starting transfers between devices, shifted(): return lax.ppermute(block, axis, route)  48.5 us
    ppermute x20, waiting for transfers between devices, shifted(): return lax.ppermute(block, axis, route)  11.1 us
  transfers between devices with their start and end apart: 20, of which 5 were waited for; matrix products, arithmetic and copies ran while one was open for 1% of the time, Pallas kernels for 0%

commit v1 on v0

--- a/solution.py
+++ b/solution.py
@@ -67,7 +67,9 @@
 
     def coarse_solve(right_side, partial_value):
         amplitude, unused = absorb(lax.all_gather(right_side[None], "mod", axis=0, tiled=True))
-        total_rho = None if partial_value is None else lax.psum(partial_value, "mod")
+        total_rho = (
+            None if partial_value is None else jnp.sum(lax.all_gather(partial_value, "mod"), axis=0)
+        )
         return (amplitude, total_rho)
 
     def project(values_in, partial_value):

time: 440 us -> 704 us (1.60)
  waiting for transfers between devices: 11.1 us -> 279 us
  blocking collectives: 356 us -> 338 us
  between operations: 0.82 us -> 14.2 us
    unnamed x0 -> x2, waiting for transfers between devices: none -> 273 us
    all_gather x3, blocking collectives: 252 us -> 235 us  [coarse_solve(): lax.all_gather(right_side[None], 'mod', axis=0, tiled=True)]
  transfers between devices with their start and end apart: 20 -> 21, of which waited for: 5 -> 5; matrix products, arithmetic and copies ran while one was open for 1% -> 1% of each run, Pallas kernels for 0% -> 0%
where the time goes in v1:
time: 704 us; the launch traced here: 703 us
  blocking collectives  338 us (48%)
  waiting for transfers between devices  279 us (40%)
  starting transfers between devices  46.6 us (7%)
  matrix products  15.1 us (2%)
  between operations  14.2 us (2%)
  local copies, waits for them, and re-layouts  7.89 us (1%)
    unnamed x2, waiting for transfers between devices  273 us
    all_gather x3, blocking collectives, coarse_solve(): lax.all_gather(right_side[None], 'mod', axis=0, tiled=True)  235 us
    psum x1, blocking collectives, on_device(): lax.psum(jnp.sum(lifted.astype(jnp.float32) * response, axis=1), 'mod')  103 us
    ppermute x20, starting transfers between devices, shifted(): return lax.ppermute(block, axis, route)  46.6 us
  transfers between devices with their start and end apart: 21, of which 5 were waited for; matrix products, arithmetic and copies ran while one was open for 1% of the time, Pallas kernels for 0%

profile of v1, /device:TPU:1, one launch (start us, length us, event | category | flops | bytes accessed | tf_op | source)
XLA Modules:
  0.0 703.1 jit_solution(1641483591612411337)
XLA Ops:
  7.5 3.6 reshape.144
  11.1 2.0 copy.8
  13.3 79.2 %all-gather.4 = f32[512,6,32]{2,1,0:T(8,128)S(1)} all-gather(f32[1,6,32]{2,1,0:T(8,128)S(1)} %convolution_bitcast_fusion.22), channel_id=2, replica_groups=mesh['mod'=512] {'mod'}, dimensions={0}, use_global_device_ids=true | all-gather | bytes 393984 | tf_op jit(solution)/shard_map/all_gather | solution.py:69
  95.8 2.4 collective-permute-start.1
  98.3 4.3 collective-permute-start.3
  102.8 2.0 collective-permute-start
  105.7 2.3 collective-permute-done
  109.6 1.9 collective-permute-start.7
  112.9 2.2 collective-permute-start.5
  115.1 3.6 collective-permute-start.4
  120.8 86.7 %all-gather.5 = f32[512,6,32]{2,1,0:T(8,128)S(1)} all-gather(f32[1,6,32]{2,1,0:T(8,128)S(1)} %convolution_bitcast_fusion.21), channel_id=3, replica_groups=mesh['mod'=512] {'mod'}, dimensions={0}, use_global_device_ids=true | all-gather | bytes 393984 | tf_op jit(solution)/shard_map/all_gather | solution.py:69
  209.7 1.9 collective-permute-start.9
  212.9 4.0 collective-permute-start.11
  216.9 3.0 collective-permute-start.8
  223.9 1.9 collective-permute-start.15
  227.2 2.2 collective-permute-start.13
  229.4 2.3 collective-permute-start.12
  232.8 272.8 %all-reduce.3.cloned.1.call-done = f32[16384]{0:T(1024)} async-done(((f32[16384]{0:T(1024)}), f32[16384]{0:T(1024)}) %all-reduce.3.cloned.1.call-update) | async-done | bytes 65552
  507.8 69.1 %all-gather.6 = f32[512,6,32]{2,1,0:T(8,128)S(1)} all-gather(f32[1,6,32]{2,1,0:T(8,128)S(1)} %convolution_bitcast_fusion.20), channel_id=5, replica_groups=mesh['mod'=512] {'mod'}, dimensions={0}, use_global_device_ids=true | all-gather | bytes 393984 | tf_op jit(solution)/shard_map/all_gather | solution.py:69
  580.5 1.9 collective-permute-start.17
  582.4 4.0 collective-permute-start.19
  586.4 2.7 collective-permute-start.16
  590.1 1.6 collective-permute-done.16
  592.6 102.9 %psum.7 = f32[32]{0:T(128)S(1)} all-reduce(f32[32]{0:T(128)S(1)} %fusion.26), channel_id=1, replica_groups=mesh['mod'=512] {'mod'}, use_global_device_ids=true, to_apply=%region_3.0 | all-reduce | flops 32 | bytes 256 | tf_op jit(solution)/shard_map/psum | solution.py:91
  (120 shorter events, 28.3 us)
Async XLA Ops:
  6.5 101.8 %copy-start = (bf16[1024,1024]{1,0:T(8,128)(2,1)S(1)}, bf16[1024,1024]{1,0:T(8,128)(2,1)}, u32[]{:S(2)}) copy-start(bf16[1024,1024]{1,0:T(8,128)(2,1)} %param.8) | copy-start | bytes 6291460
  6.5 6.6 copy-start.2
  6.5 499.0 %all-reduce.3.cloned.1.call-start = ((), (), s32[]{:S(2)}) async-start(), calls=%async_computation | async-start | bytes 131072
  94.3 10.6 %collective-permute-start.2 = (f32[2,32,128]{2,0,1:T(2,128)S(1)}, f32[2,32,128]{2,0,1:T(2,128)S(1)}, u32[]{:S(2)}, u32[]{:S(2)}) collective-permute-start(f32[2,32,128]{2,0,1:T(2,128)S(1)} %fusion.62), channel_id=1, source_target_pairs={{8,0},{9,1},{10,2},{11,3},{12,4},{13,5},{14,6},{15,7},{16,8},{17,9... | collective-permute-start | bytes 98312 | tf_op jit(solution)/shard_map/ppermute | solution.py:15
  95.8 9.4 %collective-permute-start.1 = (f32[2,32,128]{2,0,1:T(2,128)S(1)}, f32[2,32,128]{2,0,1:T(2,128)S(1)}, u32[]{:S(2)}, u32[]{:S(2)}) collective-permute-start(f32[2,32,128]{2,0,1:T(2,128)S(1)} %fusion.57), channel_id=1, source_target_pairs={{0,1},{1,2},{2,3},{3,4},{4,5},{5,6},{6,7},{7,8},{8,9},{9,10},{10,1... | collective-permute-start | bytes 98312 | tf_op jit(solution)/shard_map/ppermute | solution.py:15
  98.3 7.1 %collective-permute-start.3 = (f32[2,32,128]{2,0,1:T(2,128)S(1)}, f32[2,32,128]{2,0,1:T(2,128)S(1)}, u32[]{:S(2)}, u32[]{:S(2)}) collective-permute-start(f32[2,32,128]{2,0,1:T(2,128)S(1)} %fusion.67), channel_id=1, source_target_pairs={{0,8},{1,9},{2,10},{3,11},{4,12},{5,13},{6,14},{7,15},{8,16},{9,17... | collective-permute-start | bytes 98312 | tf_op jit(solution)/shard_map/ppermute | solution.py:15
  102.8 5.2 collective-permute-start
  109.6 9.1 %collective-permute-start.7 = (f32[2,32,128]{2,0,1:T(2,128)S(1)}, f32[2,32,128]{2,0,1:T(2,128)S(1)}, u32[]{:S(2)}, u32[]{:S(2)}) collective-permute-start(f32[2,32,128]{2,0,1:T(2,128)S(1)} %fusion.66), channel_id=1, source_target_pairs={{0,8},{1,9},{2,10},{3,11},{4,12},{5,13},{6,14},{7,15},{8,16},{9,17... | collective-permute-start | bytes 98312 | tf_op jit(solution)/shard_map/ppermute | solution.py:15
  111.6 7.5 %collective-permute-start.6 = (f32[2,32,128]{2,0,1:T(2,128)S(1)}, f32[2,32,128]{2,0,1:T(2,128)S(1)}, u32[]{:S(2)}, u32[]{:S(2)}) collective-permute-start(f32[2,32,128]{2,0,1:T(2,128)S(1)} %fusion.61), channel_id=1, source_target_pairs={{8,0},{9,1},{10,2},{11,3},{12,4},{13,5},{14,6},{15,7},{16,8},{17,9... | collective-permute-start | bytes 98312 | tf_op jit(solution)/shard_map/ppermute | solution.py:15
  112.9 6.4 collective-permute-start.5
  115.1 5.2 collective-permute-start.4
  208.5 14.0 %copy-start.1 = (bf16[1024,1024]{1,0:T(8,128)(2,1)S(1)}, bf16[1024,1024]{1,0:T(8,128)(2,1)}, u32[]{:S(2)}) copy-start(bf16[1024,1024]{1,0:T(8,128)(2,1)} %param.9) | copy-start | bytes 6291460
  209.7 10.3 %collective-permute-start.9 = (f32[2,32,128]{2,0,1:T(2,128)S(1)}, f32[2,32,128]{2,0,1:T(2,128)S(1)}, u32[]{:S(2)}, u32[]{:S(2)}) collective-permute-start(f32[2,32,128]{2,0,1:T(2,128)S(1)} %fusion.55), channel_id=1, source_target_pairs={{0,1},{1,2},{2,3},{3,4},{4,5},{5,6},{6,7},{7,8},{8,9},{9,10},{10,1... | collective-permute-start | bytes 98312 | tf_op jit(solution)/shard_map/ppermute | solution.py:15
  211.6 8.7 %collective-permute-start.10 = (f32[2,32,128]{2,0,1:T(2,128)S(1)}, f32[2,32,128]{2,0,1:T(2,128)S(1)}, u32[]{:S(2)}, u32[]{:S(2)}) collective-permute-start(f32[2,32,128]{2,0,1:T(2,128)S(1)} %fusion.60), channel_id=1, source_target_pairs={{8,0},{9,1},{10,2},{11,3},{12,4},{13,5},{14,6},{15,7},{16,8},{17,9... | collective-permute-start | bytes 98312 | tf_op jit(solution)/shard_map/ppermute | solution.py:15
  212.9 7.6 %collective-permute-start.11 = (f32[2,32,128]{2,0,1:T(2,128)S(1)}, f32[2,32,128]{2,0,1:T(2,128)S(1)}, u32[]{:S(2)}, u32[]{:S(2)}) collective-permute-start(f32[2,32,128]{2,0,1:T(2,128)S(1)} %fusion.65), channel_id=1, source_target_pairs={{0,8},{1,9},{2,10},{3,11},{4,12},{5,13},{6,14},{7,15},{8,16},{9,17... | collective-permute-start | bytes 98312 | tf_op jit(solution)/shard_map/ppermute | solution.py:15
  216.9 5.2 collective-permute-start.8
  223.9 282.6 %collective-permute-start.15 = (f32[2,32,128]{2,0,1:T(2,128)S(1)}, f32[2,32,128]{2,0,1:T(2,128)S(1)}, u32[]{:S(2)}, u32[]{:S(2)}) collective-permute-start(f32[2,32,128]{2,0,1:T(2,128)S(1)} %fusion.64), channel_id=1, source_target_pairs={{0,8},{1,9},{2,10},{3,11},{4,12},{5,13},{6,14},{7,15},{8,16},{9,17... | collective-permute-start | bytes 98312 | tf_op jit(solution)/shard_map/ppermute | solution.py:15
  225.9 281.0 %collective-permute-start.14 = (f32[2,32,128]{2,0,1:T(2,128)S(1)}, f32[2,32,128]{2,0,1:T(2,128)S(1)}, u32[]{:S(2)}, u32[]{:S(2)}) collective-permute-start(f32[2,32,128]{2,0,1:T(2,128)S(1)} %fusion.59), channel_id=1, source_target_pairs={{8,0},{9,1},{10,2},{11,3},{12,4},{13,5},{14,6},{15,7},{16,8},{17,9... | collective-permute-start | bytes 98312 | tf_op jit(solution)/shard_map/ppermute | solution.py:15
  227.2 279.9 %collective-permute-start.13 = (f32[2,32,128]{2,0,1:T(2,128)S(1)}, f32[2,32,128]{2,0,1:T(2,128)S(1)}, u32[]{:S(2)}, u32[]{:S(2)}) collective-permute-start(f32[2,32,128]{2,0,1:T(2,128)S(1)} %fusion.54), channel_id=1, source_target_pairs={{0,1},{1,2},{2,3},{3,4},{4,5},{5,6},{6,7},{7,8},{8,9},{9,10},{10,1... | collective-permute-start | bytes 98312 | tf_op jit(solution)/shard_map/ppermute | solution.py:15
  229.4 278.0 %collective-permute-start.12 = (f32[2,32,128]{2,0,1:T(2,128)S(1)}, f32[2,32,128]{2,0,1:T(2,128)S(1)}, u32[]{:S(2)}, u32[]{:S(2)}) collective-permute-start(f32[2,32,128]{2,0,1:T(2,128)S(1)} %fusion.49), channel_id=1, source_target_pairs={{1,0},{2,1},{3,2},{4,3},{5,4},{6,5},{7,6},{8,7},{9,8},{10,9},{11,1... | collective-permute-start | bytes 98312 | tf_op jit(solution)/shard_map/ppermute | solution.py:15
  579.2 10.0 %collective-permute-start.18 = (f32[2,32,128]{2,0,1:T(2,128)S(1)}, f32[2,32,128]{2,0,1:T(2,128)S(1)}, u32[]{:S(2)}, u32[]{:S(2)}) collective-permute-start(f32[2,32,128]{2,0,1:T(2,128)S(1)} %fusion.58), channel_id=1, source_target_pairs={{8,0},{9,1},{10,2},{11,3},{12,4},{13,5},{14,6},{15,7},{16,8},{17,9... | collective-permute-start | bytes 98312 | tf_op jit(solution)/shard_map/ppermute | solution.py:15
  580.5 9.0 %collective-permute-start.17 = (f32[2,32,128]{2,0,1:T(2,128)S(1)}, f32[2,32,128]{2,0,1:T(2,128)S(1)}, u32[]{:S(2)}, u32[]{:S(2)}) collective-permute-start(f32[2,32,128]{2,0,1:T(2,128)S(1)} %fusion.53), channel_id=1, source_target_pairs={{0,1},{1,2},{2,3},{3,4},{4,5},{5,6},{6,7},{7,8},{8,9},{9,10},{10,1... | collective-permute-start | bytes 98312 | tf_op jit(solution)/shard_map/ppermute | solution.py:15
  582.4 7.4 %collective-permute-start.19 = (f32[2,32,128]{2,0,1:T(2,128)S(1)}, f32[2,32,128]{2,0,1:T(2,128)S(1)}, u32[]{:S(2)}, u32[]{:S(2)}) collective-permute-start(f32[2,32,128]{2,0,1:T(2,128)S(1)} %fusion.63), channel_id=1, source_target_pairs={{0,8},{1,9},{2,10},{3,11},{4,12},{5,13},{6,14},{7,15},{8,16},{9,17... | collective-permute-start | bytes 98312 | tf_op jit(solution)/shard_map/ppermute | solution.py:15
  586.4 5.2 collective-permute-start.16
  (2 other events, 7.3 us)
Sparse Core Ops, SparseCore 0:
  232.8 272.7 all-reduce.2
